TPU v7x, 32 devices: a whole 2x2x4 slice. The times are simulated.
32 devices in a mesh: vec: 4 (over y, x), orb: 8 (over z, core).
Axes of the slice: x: 2, y: 2, z: 4, core: 2. Of those that a mesh axis runs over, the one named last changes fastest.
Arguments:
- chol_occ: float32 [44, 96, 1056], P('vec', 'orb'), may hold values from -6 to 6
- chol_vir: float32 [44, 960, 1056], P('vec', 'orb'), may hold values from -6 to 6
- singles: float32 [96, 960], P('orb'), may hold values from -0.6 to 0.6
Outputs:
- dressed_vir: float32 [44, 960, 1056], P('vec', 'orb')
- dressed_ov: float32 [44, 96, 960], P(None, 'orb', 'vec')
- fock_ov: float32 [96, 960], P('orb')
All inputs are finite; a program needn't handle non-finite values.
Results may differ from a plain program's by a relative error of at most 0.000086.
Values sent between devices are 32-bit elements; how exact they have to be, the bound alone decides.
A program may use at most 64 MiB of HBM per device.

v0:
```python
import jax
import jax.numpy as jnp
from jax import lax
from jax.sharding import PartitionSpec as P


def dress_right(matrix_rows, amplitudes):
    occ_width = amplitudes.shape[0]
    occ_cols = matrix_rows[:, :, :occ_width]
    extra_term = jnp.einsum("qrj,ja->qra", occ_cols, amplitudes, precision=lax.Precision.HIGHEST)
    return jnp.concatenate([occ_cols, matrix_rows[:, :, occ_width:] + extra_term], axis=2)


def dress_left(vir_rows, occ_all, amp_cols):
    return vir_rows - jnp.einsum("qin,ia->qan", occ_all, amp_cols, precision=lax.Precision.HIGHEST)


def shards(chol_occ, chol_vir, singles):
    amplitudes = lax.all_gather(singles, "orb", axis=0, tiled=True)
    occ_width = amplitudes.shape[0]
    vir_local = chol_vir.shape[1]
    vir_start = lax.axis_index("orb") * vir_local
    amp_cols = lax.dynamic_slice_in_dim(amplitudes, vir_start, vir_local, 1)
    occ_all = lax.all_gather(chol_occ, "orb", axis=1, tiled=True)
    dressed_vir = dress_right(dress_left(chol_vir, occ_all, amp_cols), amplitudes)
    dressed_occ = dress_right(chol_occ, amplitudes)
    local_rows = chol_occ.shape[1]
    first_row = lax.axis_index("orb") * local_rows
    row_ids = lax.broadcasted_iota(jnp.int32, (local_rows, chol_occ.shape[2]), 0) + first_row
    col_ids = lax.broadcasted_iota(jnp.int32, (local_rows, chol_occ.shape[2]), 1)
    diag_mask = jnp.where(row_ids == col_ids, 1.0, 0.0).astype(jnp.float32)
    traces_local = jnp.sum(chol_occ * diag_mask[None], axis=(1, 2))
    traces = lax.psum(traces_local, "orb")
    ov_block = dressed_occ[:, :, occ_width:]
    total_vectors = chol_occ.shape[0] * lax.axis_size("vec")
    fock_part = (
        jnp.einsum("q,qia->ia", traces, ov_block, precision=lax.Precision.HIGHEST) / total_vectors
    )
    fock_ov = lax.psum(fock_part, "vec")
    pair_blocks = lax.all_to_all(ov_block, "vec", split_axis=2, concat_axis=0, tiled=True)
    return (dressed_vir, pair_blocks, fock_ov)


def solution(mesh):
    return jax.shard_map(
        shards,
        mesh=mesh,
        in_specs=(P("vec", "orb", None), P("vec", "orb", None), P("orb", None)),
        out_specs=(P("vec", "orb", None), P(None, "orb", "vec"), P("orb", None)),
        check_vma=False,
    )
```

profile of v0, /device:TPU:0, one launch (start us, length us, event | category | flops | bytes accessed | tf_op | source)
XLA Modules:
  0.0 127.6 jit_solution(5254257879419233849)
XLA Ops:
  7.2 0.0 all-gather.3.cloned.1.call-start
  7.2 2.3 %copy.10 = f32[11,12,1056]{2,0,1:T(8,128)} copy(f32[11,12,1056]{2,1,0:T(8,128)} %param.3) | data formatting | bytes 1115136 | tf_op args[0]
  9.5 0.0 all-gather.3.cloned.1.call-update
  9.5 16.7 %all-gather = f32[8,12,960]{2,1,0:T(8,128)S(1)} all-gather(f32[1,12,960]{2,1,0:T(8,128)} %bitcast.22), channel_id=1, replica_groups=mesh['vec'=4,'orb'=8] {'orb'}, dimensions={0}, use_global_device_ids=true | all-gather | bytes 414720 | tf_op jit(solution)/shard_map/all_gather | solution.py:19
  26.3 1.9 %convolution_add_fusion = f32[11,12,960]{2,1,0:T(8,128)S(1)} fusion(f32[96,960,1]{1,0,2:T(8,128)S(1)} %reshape.23, f32[11,12,1056]{2,1,0:T(8,128)} %param.3), kind=kOutput, calls=%fused_computation.4 | convolution fusion | flops 146108160 | bytes 1433088 | tf_op jit(solution)/shard_map/qrj,ja->qra/dot_general | solution.py:10
  28.2 6.0 %copy.13 = f32[11,12,960]{1,0,2:T(8,128)} copy(f32[11,12,960]{2,1,0:T(8,128)S(1)} %convolution_add_fusion) | data formatting | bytes 1013760 | tf_op jit(solution)/shard_map/add | solution.py:11
  34.2 0.0 copy-start
  34.2 6.5 %reshape.27 = f32[4,1,31680]{2,1,0:T(1,128)} reshape(f32[960,11,12]{2,1,0:T(8,128)} %bitcast.20) | data formatting | bytes 1013760
  40.7 0.1 fusion.4
  40.8 0.0 copy-done
  40.8 0.2 multiply_reduce_fusion
  41.0 3.7 %all-to-all-start = ((f32[4,1,31680]{2,1,0:T(1,128)}), f32[4,1,31680]{2,1,0:T(1,128)S(1)}, u32[]{:S(2)}, u32[]{:S(2)}) async-start(f32[4,1,31680]{2,1,0:T(1,128)} %reshape.27), calls=%async_computation | async-start | bytes 1015808 | tf_op jit(solution)/shard_map/all_to_all | solution.py:40
  44.7 19.3 %psum.14 = f32[11]{0:T(128)S(1)} all-reduce(f32[11]{0:T(128)S(1)} %multiply_reduce_fusion), channel_id=1, replica_groups=mesh['vec'=4,'orb'=8] {'orb'}, use_global_device_ids=true, to_apply=%region_1.2 | all-reduce | flops 11 | bytes 88 | tf_op jit(solution)/shard_map/psum | solution.py:33
  64.0 0.8 fusion.1
  64.9 17.7 %psum.15 = f32[12,960]{1,0:T(8,128)} all-reduce(f32[12,960]{1,0:T(8,128)S(1)} %bitcast_multiply_fusion), channel_id=1, replica_groups=mesh['vec'=4,'orb'=8] {'vec'}, use_global_device_ids=true, to_apply=%region_2.3 | all-reduce | flops 11520 | bytes 92160 | tf_op jit(solution)/shard_map/psum | solution.py:39
  82.5 0.0 all-to-all-done
  82.5 0.5 broadcast.18
  83.0 2.1 %reduce = f32[4,31680]{1,0:T(4,128)S(1)} reduce(f32[4,1,31680]{2,1,0:T(1,128)S(1)} %all-to-all-done, f32[]{:T(128)} %broadcast.18), dimensions={1}, to_apply=%all_to_all.13.reduce_sub_computation | reduce | bytes 1013764 | tf_op jit(solution)/shard_map/all_to_all | solution.py:40
  85.2 6.0 %reshape.28 = f32[960,11,12]{2,1,0:T(8,128)} reshape(f32[4,31680]{1,0:T(4,128)S(1)} %reduce) | data formatting | bytes 1013760
  91.2 6.2 %copy.14 = f32[11,12,4,240]{3,0,2,1:T(8,128)S(1)} copy(f32[11,12,4,240]{1,0,3,2:T(8,128)} %bitcast.19) | data formatting | bytes 1013760 | tf_op jit(solution)/shard_map/all_to_all | solution.py:40
  97.4 0.9 all_to_all.16
  98.3 0.0 all-gather.3.cloned.1.call-done
  98.3 14.5 %bitcast_subtract_fusion = f32[11,120,1056]{1,2,0:T(8,128)S(1)} fusion(f32[11,120,1056]{1,2,0:T(8,128)} %param.4, f32[11,96,1056]{2,0,1:T(8,128)} %all-gather.3.cloned.1.call-done, f32[96,960]{1,0:T(8,128)S(1)} %reshape.21, s32[]{:T(128)S(6)} %select_n.11), kind=kOutput, calls=%fused_computation.1 | convolution fusion | flops 1607189760 | bytes 15661060 | tf_op jit(solution)/shard_map/qin,ia->qan/dot_general | solution.py:15
  112.9 4.7 %slice_add_fusion = f32[11,120,960]{1,2,0:T(8,128)S(1)} fusion(f32[11,120,1056]{1,2,0:T(8,128)S(1)} %bitcast_subtract_fusion, f32[96,960,1]{1,0,2:T(8,128)S(1)} %reshape.23), kind=kOutput, calls=%fused_computation.2 | convolution fusion | flops 1461081600 | bytes 11013120 | tf_op jit(solution)/shard_map/qrj,ja->qra/dot_general | solution.py:10
  117.6 3.2 %pad_maximum_fusion = f32[11,120,1056]{1,2,0:T(8,128)} fusion(f32[11,120,960]{1,2,0:T(8,128)S(1)} %slice_add_fusion, f32[11,120,96]{1,2,0:T(8,128)S(1)} %slice.16), kind=kLoop, calls=%fused_computation | loop fusion | flops 1393920 | bytes 11151360 | tf_op jit(solution)/shard_map/concatenate | solution.py:11
  (5 shorter events, 0.1 us)
Async XLA Ops:
  7.2 91.1 %all-gather.3.cloned.1.call-start = ((), (), s32[]{:S(2)}) async-start(), calls=%async_computation.1 | async-start | bytes 7962624 | tf_op jit(solution)/shard_map/all_gather | solution.py:24
  34.2 6.6 %copy-start = (f32[11,12,1056]{2,1,0:T(8,128)S(1)}, f32[11,12,1056]{2,1,0:T(8,128)}, u32[]{:S(2)}) copy-start(f32[11,12,1056]{2,1,0:T(8,128)} %param.3) | copy-start | bytes 1672708
  41.0 41.6 %all-to-all-start = ((f32[4,1,31680]{2,1,0:T(1,128)}), f32[4,1,31680]{2,1,0:T(1,128)S(1)}, u32[]{:S(2)}, u32[]{:S(2)}) async-start(f32[4,1,31680]{2,1,0:T(1,128)} %reshape.27), calls=%async_computation | async-start | bytes 1015808 | tf_op jit(solution)/shard_map/all_to_all | solution.py:40
Sparse Core Ops, SparseCore 0:
  10.2 74.4 all-gather.2
where the time goes:
time: 128 us
  blocking collectives  53.7 us (42%)
  local copies, waits for them, and re-layouts  28.5 us (22%)
  matrix products  22 us (17%)
  between operations  14.1 us (11%)
  other arithmetic  5.58 us (4%)
  starting transfers between devices  3.76 us (3%)
    psum x1, blocking collectives, shards(): traces = lax.psum(traces_local, 'orb')  19.3 us
    psum x1, blocking collectives, shards(): fock_ov = lax.psum(fock_part, 'vec')  17.7 us
    all_gather x1, blocking collectives, shards(): amplitudes = lax.all_gather(singles, 'orb', axis=0, tiled=True)  16.7 us
    unnamed x7, local copies, waits for them, and re-layouts  14.9 us
    dot_general x1, matrix products, dress_left(): jnp.einsum('qin,ia->qan', occ_all, amp_cols, precision=lax.Precision.HIGH...  14.5 us
    all_to_all x3, local copies, waits for them, and re-layouts, shards(): lax.all_to_all(ov_block, 'vec', split_axis=2, concat_axis=0, tiled=True)  7.57 us
    dot_general x2, matrix products, dress_right(): jnp.einsum('qrj,ja->qra', occ_cols, amplitudes, precision=lax.Precision.H...  6.66 us
    add x1, local copies, waits for them, and re-layouts, dress_right(): matrix_rows[:, :, occ_width:] + extra_term  5.96 us
  transfers between devices with their start and end apart: 2, of which 0 were waited for; matrix products, arithmetic and copies ran while one was open for 24% of the time, Pallas kernels for 0%

commit v1 on v0

v1 whole, which is shorter than its diff:
```python
import jax
import jax.numpy as jnp
from jax import lax
from jax.experimental import pallas as pl
from jax.experimental.pallas import tpu as pltpu
from jax.sharding import PartitionSpec as P

MESH = pl.DeviceIdType.MESH
F32, BF16 = jnp.float32, jnp.bfloat16
LANES = 128
CORES = 2


def split(x):
    hi = x.astype(BF16)
    return hi, (x - hi.astype(F32)).astype(BF16)


def dot(a, b):
    return jnp.dot(a, b, preferred_element_type=F32)


def make_kernel(W, D, Q, R, RV, N, A):
    OCC = N - A
    NZ = D // CORES
    GR = 8 if R % 8 == 0 else (4 if R % 4 == 0 else R)
    NJ = R // GR
    ROWS = Q * R
    GRAN = Q * NJ
    MAIN = N // LANES * LANES
    TAIL = N - MAIN
    SLOTS = LANES // TAIL if TAIL else 1
    GROUPS = -(-Q // SLOTS)
    PIECE = A // W
    KP = -(-OCC // LANES) * LANES
    UNITS = Q + 2

    def kernel(occ, vir, sing, out_vir, out_ov, out_fock,
               gath, amps, tails, vloc, oloc, sloc, xbuf, rows, drows, tmat, sleft,
               ovsend, ovrecv, ovout, fbuf, fout,
               s_right, s_left, s_part, r_sem, ov_s, ov_r, f_s, f_r, in_sem, v_in, v_out, o_out):
        v = lax.axis_index("vec")
        o = lax.axis_index("orb")
        z = o // CORES
        k = o % CORES
        has_r = z < NZ - 1
        has_l = z > 0
        right = lax.rem(o + CORES, D)
        left = lax.rem(o - CORES + D, D)
        part = z * CORES + (1 - k)

        c_occ = pltpu.make_async_copy(occ, oloc, in_sem.at[0])
        c_sing = pltpu.make_async_copy(sing, sloc, in_sem.at[1])
        c_occ.start()
        c_sing.start()

        def vin(q):
            return pltpu.make_async_copy(vir.at[q], vloc.at[q], v_in.at[q])

        def vout(q):
            return pltpu.make_async_copy(vloc.at[q], out_vir.at[q], v_out.at[q])

        @pl.loop(0, Q)
        def _(q):
            vin(q).start()

        bar = pltpu.get_barrier_semaphore()

        @pl.when(has_r)
        def _():
            pl.semaphore_signal(bar, inc=1, device_id=(v, right), device_id_type=MESH)

        @pl.when(has_l)
        def _():
            pl.semaphore_signal(bar, inc=1, device_id=(v, left), device_id_type=MESH)

        pl.semaphore_signal(bar, inc=1, device_id=(v, part), device_id_type=MESH)
        for h in range(1, W):
            pl.semaphore_signal(bar, inc=1, device_id=(lax.rem(v + h, W), o), device_id_type=MESH)

        c_occ.wait()
        c_sing.wait()
        for j in range(NJ):
            amps[o, j] = sloc[j * GR:(j + 1) * GR, :]
        for q in range(Q):
            for j in range(NJ):
                gath[o, q * NJ + j] = oloc[q, j * GR:(j + 1) * GR, 0:MAIN]
            rows[q * R:(q + 1) * R, 0:OCC] = oloc[q, :, 0:OCC]
        if TAIL:
            for g in range(GROUPS):
                parts = [oloc[min(g * SLOTS + t, Q - 1), :, MAIN:N] for t in range(SLOTS)]
                packed = jnp.concatenate(parts, axis=1) if SLOTS > 1 else parts[0]
                for j in range(NJ):
                    tails[o, g * NJ + j, :, 0:SLOTS * TAIL] = packed[j * GR:(j + 1) * GR]
        ri = lax.broadcasted_iota(jnp.int32, (R, KP), 0) + o * R
        ci = lax.broadcasted_iota(jnp.int32, (R, KP), 1)
        mask = ri == ci
        lane = lax.broadcasted_iota(jnp.int32, (GR, LANES), 1)
        tr = jnp.zeros((GR, LANES), F32)
        for q in range(Q):
            dq = jnp.sum(jnp.where(mask, oloc[q, :, 0:KP], 0.0), axis=0, keepdims=True)
            tq = jnp.sum(dq, axis=1, keepdims=True)
            tr = tr + jnp.where(lane == q, jnp.broadcast_to(tq, (GR, LANES)), 0.0)
        tails[o, GROUPS * NJ] = tr

        pl.semaphore_wait(bar, has_r.astype(jnp.int32) + has_l.astype(jnp.int32) + W)

        def piece(d, u):
            if isinstance(u, str):
                return {"a": amps, "t": tails}[u].at[d], {"a": Q, "t": Q + 1}[u]
            return gath.at[d, pl.ds(u * NJ, NJ)], u

        def remote(d, u, sems, target):
            ref, i = piece(d, u)
            return pltpu.make_async_remote_copy(
                src_ref=ref, dst_ref=ref, send_sem=sems.at[d, i], recv_sem=r_sem.at[d, i],
                device_id=(v, target), device_id_type=MESH)

        def send_own(u):
            @pl.when(has_r)
            def _():
                remote(o, u, s_right, right).start()

            @pl.when(has_l)
            def _():
                remote(o, u, s_left, left).start()

            remote(o, u, s_part, part).start()

        def relay(u):
            for h in range(1, NZ):
                @pl.when(z - h >= 0)
                def _():
                    d = (z - h) * CORES + k
                    remote(d, u, s_right, right).wait_recv()

                    @pl.when(has_r)
                    def _():
                        remote(d, u, s_right, right).start()

                    remote(d, u, s_part, part).start()

                @pl.when(z + h < NZ)
                def _():
                    d = (z + h) * CORES + k
                    remote(d, u, s_left, left).wait_recv()

                    @pl.when(has_l)
                    def _():
                        remote(d, u, s_left, left).start()

                    remote(d, u, s_part, part).start()

            for s in range(NZ):
                remote(s * CORES + 1 - k, u, s_part, part).wait_recv()

        def finish(u):
            for s in range(NZ):
                d = s * CORES + k

                @pl.when(jnp.logical_and(s <= z, has_r))
                def _():
                    remote(d, u, s_right, right).wait_send()

                @pl.when(jnp.logical_and(s >= z, has_l))
                def _():
                    remote(d, u, s_left, left).wait_send()

                remote(d, u, s_part, part).wait_send()

        send_own("a")
        send_own("t")

        @pl.loop(0, Q)
        def _(u):
            send_own(u)

        relay("a")
        relay("t")

        for d in range(D):
            for j in range(NJ):
                at = d * R + j * GR
                xbuf[at:at + GR, 0:A] = amps[d, j]
        amp = xbuf[:, 0:A]
        tmat[...] = jnp.zeros_like(tmat)
        shifted = jnp.concatenate([jnp.zeros((OCC, OCC), F32), amp], axis=1)
        thi, tlo = split(shifted)
        tmat[0:OCC, :] = thi
        tmat[KP:KP + OCC, :] = tlo
        ahi, alo = split(amp)
        pick = (lax.broadcasted_iota(jnp.int32, (RV, A), 1)
                == lax.broadcasted_iota(jnp.int32, (RV, A), 0) + o * RV)
        pick = jnp.where(pick, 1.0, 0.0).astype(BF16)

        def take(x):
            return lax.dot_general(pick, x, (((1,), (1,)), ((), ())), preferred_element_type=F32)

        sleft[0, :, 0:OCC] = take(ahi).astype(BF16)
        sleft[1, :, 0:OCC] = take(alo).astype(BF16)

        def dress(x):
            hi, lo = split(x)
            return dot(jnp.concatenate([hi, hi], axis=1), tmat[...]) + dot(lo, tmat[0:KP, :])

        keep = lax.broadcasted_iota(jnp.int32, (ROWS, KP), 1) < OCC
        extra = dress(jnp.where(keep, rows[...], 0.0))
        for q in range(Q):
            drows[q * R:(q + 1) * R, :] = oloc[q] + extra[q * R:(q + 1) * R]
        for w in range(W):
            sl = drows[:, OCC + w * PIECE:OCC + (w + 1) * PIECE]
            for g in range(GRAN):
                ovsend[w, g] = sl[g * GR:(g + 1) * GR]
        total = tails[0, GROUPS * NJ]
        for d in range(1, D):
            total = total + tails[d, GROUPS * NJ]
        fock = jnp.zeros((R, N), F32)
        for q in range(Q):
            fock = fock + total[0:1, q:q + 1] * drows[q * R:(q + 1) * R, :]
        fock = fock[:, OCC:]
        for j in range(NJ):
            fbuf[v, j] = fock[j * GR:(j + 1) * GR]

        def ov_copy(h):
            w = lax.rem(v + h, W)
            return pltpu.make_async_remote_copy(
                src_ref=ovsend.at[w], dst_ref=ovrecv.at[v], send_sem=ov_s.at[h],
                recv_sem=ov_r.at[h], device_id=(w, o), device_id_type=MESH)

        def f_copy(h):
            w = lax.rem(v + h, W)
            return pltpu.make_async_remote_copy(
                src_ref=fbuf.at[v], dst_ref=fbuf.at[v], send_sem=f_s.at[h],
                recv_sem=f_r.at[h], device_id=(w, o), device_id_type=MESH)

        for h in range(1, W):
            ov_copy(h).start()
            f_copy(h).start()
        ovrecv[v] = ovsend[v]

        shi = sleft[0, :, 0:OCC]
        slo = sleft[1, :, 0:OCC]

        @pl.loop(0, Q)
        def _(q):
            relay(q)
            if TAIL:
                shift = lax.rem(LANES - lax.rem(q, SLOTS) * TAIL, LANES)
            for d in range(D):
                for j in range(NJ):
                    at = d * R + j * GR
                    xbuf[at:at + GR, 0:MAIN] = gath[d, q * NJ + j]
                    if TAIL:
                        t = pltpu.roll(tails[d, (q // SLOTS) * NJ + j], shift, axis=1)
                        xbuf[at:at + GR, MAIN:N] = t[:, 0:TAIL]
            hi, lo = split(xbuf[...])
            prod = dot(shi, hi) + (dot(shi, lo) + dot(slo, hi))
            vin(q).wait()
            vloc[q] = vloc[q] - prod
            keep_v = lax.broadcasted_iota(jnp.int32, (RV, KP), 1) < OCC
            vloc[q] = vloc[q] + dress(jnp.where(keep_v, vloc[q, :, 0:KP], 0.0))
            vout(q).start()

        for h in range(1, W):
            ov_copy(h).wait_recv()
            f_copy(h).wait_recv()
        for w in range(W):
            for g in range(GRAN):
                j = g % NJ
                ovout[w * Q + g // NJ, j * GR:(j + 1) * GR, :] = ovrecv[w, g]
        c_ov = pltpu.make_async_copy(ovout, out_ov, o_out.at[0])
        c_ov.start()
        for j in range(NJ):
            acc = fbuf[0, j]
            for w in range(1, W):
                acc = acc + fbuf[w, j]
            fout[j * GR:(j + 1) * GR, :] = acc / (Q * W)
        c_f = pltpu.make_async_copy(fout, out_fock, o_out.at[1])
        c_f.start()

        finish("a")
        finish("t")

        @pl.loop(0, Q)
        def _(u):
            finish(u)
            vout(u).wait()

        for h in range(1, W):
            ov_copy(h).wait_send()
            f_copy(h).wait_send()
        c_ov.wait()
        c_f.wait()

    DMA = pltpu.SemaphoreType.DMA
    V = pltpu.VMEM
    any_spec = pl.BlockSpec(memory_space=pl.ANY)
    return pl.pallas_call(
        kernel,
        name="dress",
        out_shape=(jax.ShapeDtypeStruct((Q, RV, N), F32),
                   jax.ShapeDtypeStruct((Q * W, R, PIECE), F32),
                   jax.ShapeDtypeStruct((R, A), F32)),
        in_specs=[any_spec] * 3,
        out_specs=(any_spec,) * 3,
        scratch_shapes=[
            V((D, GRAN, GR, MAIN), F32),
            V((D, NJ, GR, A), F32),
            V((D, GROUPS * NJ + 1, GR, LANES), F32),
            V((Q, RV, N), F32),
            V((Q, R, N), F32),
            V((R, A), F32),
            V((OCC, N), F32),
            V((ROWS, KP), F32),
            V((ROWS, N), F32),
            V((2 * KP, N), BF16),
            V((2, RV, KP), BF16),
            V((W, GRAN, GR, PIECE), F32),
            V((W, GRAN, GR, PIECE), F32),
            V((Q * W, R, PIECE), F32),
            V((W, NJ, GR, A), F32),
            V((R, A), F32),
            DMA((D, UNITS)), DMA((D, UNITS)), DMA((D, UNITS)), DMA((D, UNITS)),
            DMA((W,)), DMA((W,)), DMA((W,)), DMA((W,)),
            DMA((2,)), DMA((Q,)), DMA((Q,)), DMA((2,)),
        ],
        compiler_params=pltpu.CompilerParams(
            collective_id=0, has_side_effects=True, vmem_limit_bytes=40 * 2**20),
    )


def solution(mesh):
    W, D = mesh.shape["vec"], mesh.shape["orb"]

    def shards(chol_occ, chol_vir, singles):
        Q, R, N = chol_occ.shape
        call = make_kernel(W, D, Q, R, chol_vir.shape[1], N, singles.shape[1])
        return call(chol_occ, chol_vir, singles)

    return jax.shard_map(
        shards,
        mesh=mesh,
        in_specs=(P("vec", "orb", None), P("vec", "orb", None), P("orb", None)),
        out_specs=(P("vec", "orb", None), P(None, "orb", "vec"), P("orb", None)),
        check_vma=False,
    )
```

time: 128 us -> 108 us (0.84)
  Pallas kernels: 0 us -> 84.6 us
  blocking collectives: 53.7 us -> 0 us
  matrix products: 22 us -> 0 us
  between operations: 14.1 us -> 0.67 us
  local copies, waits for them, and re-layouts: 28.5 us -> 21.5 us
  other arithmetic: 5.58 us -> 0 us
  starting transfers between devices: 3.76 us -> 0 us
    pallas_call x0 -> x1, Pallas kernels: none -> 84.6 us  [shards(): return call(chol_occ, chol_vir, singles)]
    psum x2 -> x0, blocking collectives: 37 us -> none  [the longest x1 19.3 us: shards(): traces = lax.psum(traces_local, 'orb')]
    dot_general x4 -> x0, matrix products: 22 us -> none  [the longest x1 14.5 us: dress_left(): jnp.einsum('qin,ia->qan', occ_all, amp_cols, precision=lax.Precision.HIGH...]
    all_gather x1 -> x0, blocking collectives: 16.7 us -> none  [shards(): amplitudes = lax.all_gather(singles, 'orb', axis=0, tiled=True)]
    pallas_call x0 -> x2, local copies, waits for them, and re-layouts: none -> 8.44 us  [shards(): return call(chol_occ, chol_vir, singles)]
    all_to_all x3 -> x0, local copies, waits for them, and re-layouts: 7.57 us -> none  [shards(): lax.all_to_all(ov_block, 'vec', split_axis=2, concat_axis=0, tiled=True)]
    add x1 -> x0, local copies, waits for them, and re-layouts: 5.96 us -> none  [dress_right(): matrix_rows[:, :, occ_width:] + extra_term]
    all_to_all x1 -> x0, starting transfers between devices: 3.72 us -> none  [shards(): lax.all_to_all(ov_block, 'vec', split_axis=2, concat_axis=0, tiled=True)]
  transfers between devices with their start and end apart: 2 -> 0, of which waited for: 0 -> 0; matrix products, arithmetic and copies ran while one was open for 24% -> 0% of each run, Pallas kernels for 0% -> 0%
where the time goes in v1:
time: 108 us; the launch traced here: 107 us
  Pallas kernels  84.6 us (78%)
  local copies, waits for them, and re-layouts  21.5 us (20%)
    pallas_call x1, Pallas kernels, shards(): return call(chol_occ, chol_vir, singles)  84.6 us
    unnamed x10, local copies, waits for them, and re-layouts  13.1 us
    pallas_call x2, local copies, waits for them, and re-layouts, shards(): return call(chol_occ, chol_vir, singles)  8.44 us

profile of v1, /device:TPU:0, one launch (start us, length us, event | category | flops | bytes accessed | tf_op | source)
XLA Modules:
  0.0 106.7 jit_solution(6015167895731378688)
XLA Ops:
  0.6 0.0 copy-start.3
  0.6 0.0 copy-start.2
  0.7 7.1 %copy.6.vir = f32[11,120,1056]{2,1,0:T(8,128)} copy(f32[11,120,1056]{1,2,0:T(8,128)} %param.4) | data formatting | bytes 11151360 | tf_op args[1]
  7.8 0.0 copy-done.3
  7.8 0.0 copy-done.2
  7.8 0.0 copy-start
  7.8 2.7 %copy-done = f32[11,120,1056]{2,1,0:T(8,128)S(1)} copy-done((f32[11,120,1056]{2,1,0:T(8,128)S(1)}, f32[11,120,1056]{2,1,0:T(8,128)}, u32[]{:S(2)}) %copy-start) | copy-done | bytes 5575704
  10.5 84.6 %dress.1 = (f32[11,120,1056]{2,1,0:T(8,128)S(1)}, f32[44,12,240]{2,1,0:T(8,128)S(1)}, f32[12,960]{1,0:T(8,128)S(1)}) custom-call(f32[11,12,1056]{2,1,0:T(8,128)S(1)} %copy-done.2, f32[11,120,1056]{2,1,0:T(8,128)S(1)} %copy-done, f32[12,960]{1,0:T(8,128)S(1)} %copy-done.3), custom_call_target="tpu_custom_call" | custom-call | tf_op jit(solution)/shard_map/dress/pallas_call | solution.py:338
  95.1 0.0 copy-start.1
  95.1 2.6 %copy-done.1 = f32[11,120,1056]{2,1,0:T(8,128)} copy-done((f32[11,120,1056]{2,1,0:T(8,128)}, f32[11,120,1056]{2,1,0:T(8,128)S(1)}, u32[]{:S(2)}) %copy-start.1) | copy-done | bytes 5575704
  97.7 7.3 %copy.7 = f32[11,120,1056]{1,2,0:T(8,128)} copy(f32[11,120,1056]{2,1,0:T(8,128)} %copy-done.1) | data formatting | bytes 11151360 | tf_op jit(solution)/shard_map/dress/pallas_call | solution.py:338
  105.0 1.1 %copy.8 = f32[44,12,240]{2,0,1:T(8,128)} copy(f32[44,12,240]{2,1,0:T(8,128)S(1)} %get-tuple-element.4) | data formatting | bytes 1013760 | tf_op jit(solution)/shard_map/dress/pallas_call | solution.py:338
  106.1 0.6 copy.10
Async XLA Ops:
  0.6 7.2 %copy-start.3 = (f32[12,960]{1,0:T(8,128)S(1)}, f32[12,960]{1,0:T(8,128)}, u32[]{:S(2)}) copy-start(f32[12,960]{1,0:T(8,128)} %sing.1) | copy-start | bytes 138244
  0.6 7.2 %copy-start.2 = (f32[11,12,1056]{2,1,0:T(8,128)S(1)}, f32[11,12,1056]{2,1,0:T(8,128)}, u32[]{:S(2)}) copy-start(f32[11,12,1056]{2,1,0:T(8,128)} %occ.1) | copy-start | bytes 1672708
  7.8 2.7 %copy-start = (f32[11,120,1056]{2,1,0:T(8,128)S(1)}, f32[11,120,1056]{2,1,0:T(8,128)}, u32[]{:S(2)}) copy-start(f32[11,120,1056]{2,1,0:T(8,128)} %copy.6.vir) | copy-start | bytes 16727044
  95.1 2.6 %copy-start.1 = (f32[11,120,1056]{2,1,0:T(8,128)}, f32[11,120,1056]{2,1,0:T(8,128)S(1)}, u32[]{:S(2)}) copy-start(f32[11,120,1056]{2,1,0:T(8,128)S(1)} %get-tuple-element.3) | copy-start | bytes 16727044

commit v2 on v1

--- a/solution.py
+++ b/solution.py
@@ -34,9 +34,12 @@
     PIECE = A // W
     KP = -(-OCC // LANES) * LANES
     UNITS = Q + 2
+    NP = -(-N // LANES) * LANES
+    AP = -(-A // LANES) * LANES
+    VP = -(-RV // LANES) * LANES
 
     def kernel(occ, vir, sing, out_vir, out_ov, out_fock,
-               gath, amps, tails, vloc, oloc, sloc, xbuf, rows, drows, tmat, sleft,
+               gath, amps, tails, vloc, oloc, sloc, xbuf, drows, tmat, tright, sleft, lwts,
                ovsend, ovrecv, ovout, fbuf, fout,
                s_right, s_left, s_part, r_sem, ov_s, ov_r, f_s, f_r, in_sem, v_in, v_out, o_out):
         v = lax.axis_index("vec")
@@ -85,7 +88,6 @@
         for q in range(Q):
             for j in range(NJ):
                 gath[o, q * NJ + j] = oloc[q, j * GR:(j + 1) * GR, 0:MAIN]
-            rows[q * R:(q + 1) * R, 0:OCC] = oloc[q, :, 0:OCC]
         if TAIL:
             for g in range(GROUPS):
                 parts = [oloc[min(g * SLOTS + t, Q - 1), :, MAIN:N] for t in range(SLOTS)]
@@ -178,46 +180,53 @@
         relay("a")
         relay("t")
 
+        xbuf[...] = jnp.zeros_like(xbuf)
         for d in range(D):
             for j in range(NJ):
                 at = d * R + j * GR
                 xbuf[at:at + GR, 0:A] = amps[d, j]
-        amp = xbuf[:, 0:A]
+        amp = xbuf[0:OCC, 0:A]
         tmat[...] = jnp.zeros_like(tmat)
         shifted = jnp.concatenate([jnp.zeros((OCC, OCC), F32), amp], axis=1)
         thi, tlo = split(shifted)
         tmat[0:OCC, :] = thi
         tmat[KP:KP + OCC, :] = tlo
-        ahi, alo = split(amp)
-        pick = (lax.broadcasted_iota(jnp.int32, (RV, A), 1)
-                == lax.broadcasted_iota(jnp.int32, (RV, A), 0) + o * RV)
+        thi, tlo = split(jnp.transpose(xbuf[:, 0:AP])[0:A])
+        tright[:, 0:KP] = thi
+        tright[:, KP:2 * KP] = tlo
+        ahi, alo = split(xbuf[:, 0:A])
+        pick = (lax.broadcasted_iota(jnp.int32, (A, VP), 0)
+                == lax.broadcasted_iota(jnp.int32, (A, VP), 1) + o * RV)
         pick = jnp.where(pick, 1.0, 0.0).astype(BF16)
-
-        def take(x):
-            return lax.dot_general(pick, x, (((1,), (1,)), ((), ())), preferred_element_type=F32)
-
-        sleft[0, :, 0:OCC] = take(ahi).astype(BF16)
-        sleft[1, :, 0:OCC] = take(alo).astype(BF16)
-
-        def dress(x):
-            hi, lo = split(x)
-            return dot(jnp.concatenate([hi, hi], axis=1), tmat[...]) + dot(lo, tmat[0:KP, :])
-
+        shi = dot(ahi, pick).astype(BF16)
+        sleft[0:KP, 0:VP] = shi
+        sleft[KP:2 * KP, 0:VP] = shi
+        sleft[0:KP, VP:2 * VP] = dot(alo, pick).astype(BF16)
+        sleft[KP:2 * KP, VP:2 * VP] = jnp.zeros((KP, VP), BF16)
+        lwts[...] = jnp.zeros_like(lwts)
+
+        for q in range(Q):
+            for r in range(R):
+                drows[r * Q + q:r * Q + q + 1, :] = oloc[q, r:r + 1, :]
         keep = lax.broadcasted_iota(jnp.int32, (ROWS, KP), 1) < OCC
-        extra = dress(jnp.where(keep, rows[...], 0.0))
-        for q in range(Q):
-            drows[q * R:(q + 1) * R, :] = oloc[q] + extra[q * R:(q + 1) * R]
+        hi, lo = split(jnp.where(keep, drows[:, 0:KP], 0.0))
+        extra = dot(jnp.concatenate([hi, hi], axis=1), tmat[...]) + dot(lo, tmat[0:KP, :])
+        drows[...] = drows[...] + extra
         for w in range(W):
             sl = drows[:, OCC + w * PIECE:OCC + (w + 1) * PIECE]
-            for g in range(GRAN):
-                ovsend[w, g] = sl[g * GR:(g + 1) * GR]
+            for r in range(R):
+                ovsend[w, r] = sl[r * Q:(r + 1) * Q]
         total = tails[0, GROUPS * NJ]
         for d in range(1, D):
             total = total + tails[d, GROUPS * NJ]
-        fock = jnp.zeros((R, N), F32)
+        rid = lax.broadcasted_iota(jnp.int32, (R, ROWS), 0) * Q
+        cid = lax.broadcasted_iota(jnp.int32, (R, ROWS), 1)
+        wts = jnp.zeros((R, ROWS), F32)
         for q in range(Q):
-            fock = fock + total[0:1, q:q + 1] * drows[q * R:(q + 1) * R, :]
-        fock = fock[:, OCC:]
+            wts = wts + jnp.where(cid == rid + q, jnp.broadcast_to(total[0:1, q:q + 1], (R, ROWS)), 0.0)
+        whi, wlo = split(wts)
+        dhi, dlo = split(drows[...])
+        fock = (dot(whi, dhi) + (dot(whi, dlo) + dot(wlo, dhi)))[:, OCC:]
         for j in range(NJ):
             fbuf[v, j] = fock[j * GR:(j + 1) * GR]
 
@@ -237,9 +246,6 @@
             ov_copy(h).start()
             f_copy(h).start()
         ovrecv[v] = ovsend[v]
-
-        shi = sleft[0, :, 0:OCC]
-        slo = sleft[1, :, 0:OCC]
 
         @pl.loop(0, Q)
         def _(q):
@@ -253,21 +259,26 @@
                     if TAIL:
                         t = pltpu.roll(tails[d, (q // SLOTS) * NJ + j], shift, axis=1)
                         xbuf[at:at + GR, MAIN:N] = t[:, 0:TAIL]
-            hi, lo = split(xbuf[...])
-            prod = dot(shi, hi) + (dot(shi, lo) + dot(slo, hi))
+            hi, lo = split(jnp.transpose(xbuf[...])[0:N])
+            prod = dot(jnp.concatenate([hi, lo], axis=1), sleft[...])
+            prod = prod[:, 0:VP] + prod[:, VP:2 * VP]
             vin(q).wait()
-            vloc[q] = vloc[q] - prod
-            keep_v = lax.broadcasted_iota(jnp.int32, (RV, KP), 1) < OCC
-            vloc[q] = vloc[q] + dress(jnp.where(keep_v, vloc[q, :, 0:KP], 0.0))
+            vloc[q] = vloc[q] - prod[:, 0:RV]
+            hi, lo = split(vloc[q, 0:OCC, :])
+            lwts[0:OCC, 0:RV] = hi
+            lwts[KP:KP + OCC, 0:RV] = hi
+            lwts[0:OCC, VP:VP + RV] = lo
+            prod = dot(tright[...], lwts[...])
+            prod = prod[:, 0:VP] + prod[:, VP:2 * VP]
+            vloc[q, OCC:N, :] = vloc[q, OCC:N, :] + prod[:, 0:RV]
             vout(q).start()
 
         for h in range(1, W):
             ov_copy(h).wait_recv()
             f_copy(h).wait_recv()
         for w in range(W):
-            for g in range(GRAN):
-                j = g % NJ
-                ovout[w * Q + g // NJ, j * GR:(j + 1) * GR, :] = ovrecv[w, g]
+            for r in range(R):
+                ovout[r, w * Q:(w + 1) * Q, :] = ovrecv[w, r]
         c_ov = pltpu.make_async_copy(ovout, out_ov, o_out.at[0])
         c_ov.start()
         for j in range(NJ):
@@ -298,26 +309,27 @@
     return pl.pallas_call(
         kernel,
         name="dress",
-        out_shape=(jax.ShapeDtypeStruct((Q, RV, N), F32),
-                   jax.ShapeDtypeStruct((Q * W, R, PIECE), F32),
+        out_shape=(jax.ShapeDtypeStruct((Q, N, RV), F32),
+                   jax.ShapeDtypeStruct((R, Q * W, PIECE), F32),
                    jax.ShapeDtypeStruct((R, A), F32)),
-        in_specs=[any_spec] * 3,
+        in_specs=[pl.BlockSpec(memory_space=pltpu.HBM)] * 3,
         out_specs=(any_spec,) * 3,
         scratch_shapes=[
             V((D, GRAN, GR, MAIN), F32),
             V((D, NJ, GR, A), F32),
             V((D, GROUPS * NJ + 1, GR, LANES), F32),
-            V((Q, RV, N), F32),
+            V((Q, N, RV), F32),
             V((Q, R, N), F32),
             V((R, A), F32),
-            V((OCC, N), F32),
-            V((ROWS, KP), F32),
+            V((KP, NP), F32),
             V((ROWS, N), F32),
             V((2 * KP, N), BF16),
-            V((2, RV, KP), BF16),
-            V((W, GRAN, GR, PIECE), F32),
-            V((W, GRAN, GR, PIECE), F32),
-            V((Q * W, R, PIECE), F32),
+            V((A, 2 * KP), BF16),
+            V((2 * KP, 2 * VP), BF16),
+            V((2 * KP, 2 * VP), BF16),
+            V((W, R, Q, PIECE), F32),
+            V((W, R, Q, PIECE), F32),
+            V((R, Q * W, PIECE), F32),
             V((W, NJ, GR, A), F32),
             V((R, A), F32),
             DMA((D, UNITS)), DMA((D, UNITS)), DMA((D, UNITS)), DMA((D, UNITS)),
@@ -335,7 +347,8 @@
     def shards(chol_occ, chol_vir, singles):
         Q, R, N = chol_occ.shape
         call = make_kernel(W, D, Q, R, chol_vir.shape[1], N, singles.shape[1])
-        return call(chol_occ, chol_vir, singles)
+        vir, ov, fock = call(chol_occ, jnp.swapaxes(chol_vir, 1, 2), singles)
+        return jnp.swapaxes(vir, 1, 2), jnp.swapaxes(ov, 0, 1), fock
 
     return jax.shard_map(
         shards,

time: 108 us -> 98.1 us (0.908)
  the two profiles are of different devices: /device:TPU:0 before, /device:TPU:7 now
where the time goes in v2:
time: 98.1 us; the launch traced here: 97.8 us
  Pallas kernels  88.5 us (90%)
  local copies, waits for them, and re-layouts  8.7 us (9%)
    pallas_call x1, Pallas kernels, shards(): vir, ov, fock = call(chol_occ, jnp.swapaxes(chol_vir, 1, 2), singles)  88.5 us
    unnamed x9, local copies, waits for them, and re-layouts  8.7 us

profile of v2, /device:TPU:7, one launch (start us, length us, event | category | flops | bytes accessed | tf_op | source)
XLA Modules:
  0.0 97.8 jit_solution(1810202405918076875)
XLA Ops:
  0.6 0.0 copy-start
  0.6 2.7 %copy-done = f32[11,120,1056]{1,2,0:T(8,128)S(1)} copy-done((f32[11,120,1056]{1,2,0:T(8,128)S(1)}, f32[11,120,1056]{1,2,0:T(8,128)}, u32[]{:S(2)}) %copy-start) | copy-done | bytes 5575704
  3.3 0.0 copy-start.1
  3.3 1.1 %copy-done.1 = f32[11,12,1056]{2,1,0:T(8,128)S(1)} copy-done((f32[11,12,1056]{2,1,0:T(8,128)S(1)}, f32[11,12,1056]{2,1,0:T(8,128)}, u32[]{:S(2)}) %copy-start.1) | copy-done | bytes 557592
  4.5 0.0 copy-start.2
  4.5 0.8 copy-done.2
  5.3 88.5 %dress.1 = (f32[11,1056,120]{2,1,0:T(8,128)S(1)}, f32[12,44,240]{2,1,0:T(8,128)S(1)}, f32[12,960]{1,0:T(8,128)S(1)}) custom-call(f32[11,12,1056]{2,1,0:T(8,128)S(1)} %copy-done.1, f32[11,1056,120]{2,1,0:T(8,128)S(1)} %bitcast.3, f32[12,960]{1,0:T(8,128)S(1)} %copy-done.2), custom_call_target="tpu_custom_call" | custom-call | tf_op jit(solution)/shard_map/dress/pallas_call | solution.py:350
  93.8 2.6 %copy.9 = f32[11,120,1056]{1,2,0:T(8,128)} copy(f32[11,120,1056]{1,2,0:T(8,128)S(1)} %bitcast.4) | data formatting | bytes 11151360
  96.4 0.8 copy.10
  97.2 0.6 copy.11
Async XLA Ops:
  0.6 2.7 %copy-start = (f32[11,120,1056]{1,2,0:T(8,128)S(1)}, f32[11,120,1056]{1,2,0:T(8,128)}, u32[]{:S(2)}) copy-start(f32[11,120,1056]{1,2,0:T(8,128)} %param.4) | copy-start | bytes 16727044
  3.3 1.1 %copy-start.1 = (f32[11,12,1056]{2,1,0:T(8,128)S(1)}, f32[11,12,1056]{2,1,0:T(8,128)}, u32[]{:S(2)}) copy-start(f32[11,12,1056]{2,1,0:T(8,128)} %occ.1) | copy-start | bytes 1672708
  4.5 0.8 copy-start.2

commit v3 on v2

--- a/solution.py
+++ b/solution.py
@@ -9,6 +9,8 @@
 F32, BF16 = jnp.float32, jnp.bfloat16
 LANES = 128
 CORES = 2
+SKEW = 2
+AHEAD = 4
 
 
 def split(x):
@@ -129,32 +131,35 @@
 
             remote(o, u, s_part, part).start()
 
-        def relay(u):
-            for h in range(1, NZ):
-                @pl.when(z - h >= 0)
-                def _():
-                    d = (z - h) * CORES + k
-                    remote(d, u, s_right, right).wait_recv()
-
-                    @pl.when(has_r)
-                    def _():
-                        remote(d, u, s_right, right).start()
-
-                    remote(d, u, s_part, part).start()
-
-                @pl.when(z + h < NZ)
-                def _():
-                    d = (z + h) * CORES + k
-                    remote(d, u, s_left, left).wait_recv()
-
-                    @pl.when(has_l)
-                    def _():
-                        remote(d, u, s_left, left).start()
-
-                    remote(d, u, s_part, part).start()
-
+        def relay(h, u):
+            @pl.when(z - h >= 0)
+            def _():
+                d = (z - h) * CORES + k
+                remote(d, u, s_right, right).wait_recv()
+
+                @pl.when(has_r)
+                def _():
+                    remote(d, u, s_right, right).start()
+
+                remote(d, u, s_part, part).start()
+
+            @pl.when(z + h < NZ)
+            def _():
+                d = (z + h) * CORES + k
+                remote(d, u, s_left, left).wait_recv()
+
+                @pl.when(has_l)
+                def _():
+                    remote(d, u, s_left, left).start()
+
+                remote(d, u, s_part, part).start()
+
+        def from_partner(u):
             for s in range(NZ):
                 remote(s * CORES + 1 - k, u, s_part, part).wait_recv()
+
+        units = ["a", "t"] + list(range(Q))
+        LEAD = 2 + SKEW * max(NZ - 2, 0)
 
         def finish(u):
             for s in range(NZ):
@@ -170,15 +175,22 @@
 
                 remote(d, u, s_part, part).wait_send()
 
-        send_own("a")
-        send_own("t")
-
-        @pl.loop(0, Q)
-        def _(u):
+        for u in units[:AHEAD]:
             send_own(u)
 
-        relay("a")
-        relay("t")
+        for q in range(Q):
+            for r in range(R):
+                drows[r * Q + q:r * Q + q + 1, :] = oloc[q, r:r + 1, :]
+
+        for t in range(LEAD):
+            if AHEAD <= t + AHEAD < UNITS:
+                send_own(units[t + AHEAD])
+            for h in range(1, NZ):
+                n = t - SKEW * (h - 1)
+                if 0 <= n < UNITS:
+                    relay(h, units[n])
+        from_partner("a")
+        from_partner("t")
 
         xbuf[...] = jnp.zeros_like(xbuf)
         for d in range(D):
@@ -205,9 +217,6 @@
         sleft[KP:2 * KP, VP:2 * VP] = jnp.zeros((KP, VP), BF16)
         lwts[...] = jnp.zeros_like(lwts)
 
-        for q in range(Q):
-            for r in range(R):
-                drows[r * Q + q:r * Q + q + 1, :] = oloc[q, r:r + 1, :]
         keep = lax.broadcasted_iota(jnp.int32, (ROWS, KP), 1) < OCC
         hi, lo = split(jnp.where(keep, drows[:, 0:KP], 0.0))
         extra = dot(jnp.concatenate([hi, hi], axis=1), tmat[...]) + dot(lo, tmat[0:KP, :])
@@ -249,7 +258,18 @@
 
         @pl.loop(0, Q)
         def _(q):
-            relay(q)
+            @pl.when(q + LEAD + AHEAD < UNITS)
+            def _():
+                send_own(q + LEAD + AHEAD - 2)
+
+            for h in range(1, NZ):
+                n = q + LEAD - SKEW * (h - 1)
+
+                @pl.when(n < UNITS)
+                def _():
+                    relay(h, n - 2)
+
+            from_partner(q)
             if TAIL:
                 shift = lax.rem(LANES - lax.rem(q, SLOTS) * TAIL, LANES)
             for d in range(D):
@@ -347,7 +367,8 @@
     def shards(chol_occ, chol_vir, singles):
         Q, R, N = chol_occ.shape
         call = make_kernel(W, D, Q, R, chol_vir.shape[1], N, singles.shape[1])
-        vir, ov, fock = call(chol_occ, jnp.swapaxes(chol_vir, 1, 2), singles)
+        args = (chol_occ, jnp.swapaxes(chol_vir, 1, 2), singles)
+        vir, ov, fock = call(*(pltpu.with_memory_space_constraint(a, pltpu.HBM) for a in args))
         return jnp.swapaxes(vir, 1, 2), jnp.swapaxes(ov, 0, 1), fock
 
     return jax.shard_map(

time: 98.1 us -> 60.1 us (0.61)
  the two profiles are of different devices: /device:TPU:7 before, /device:TPU:0 now
where the time goes in v3:
time: 60.1 us; the launch traced here: 60 us
  Pallas kernels  55.3 us (92%)
  local copies, waits for them, and re-layouts  4.04 us (7%)
  between operations  0.64 us (1%)
    pallas_call x1, Pallas kernels, shards(): call(*(pltpu.with_memory_space_constraint(a, pltpu.HBM) for a in args))  55.3 us
    unnamed x3, local copies, waits for them, and re-layouts  4.04 us

profile of v3, /device:TPU:0, one launch (start us, length us, event | category | flops | bytes accessed | tf_op | source)
XLA Modules:
  0.0 60.0 jit_solution(3658300247664820737)
XLA Ops:
  0.6 55.3 %dress.1 = (f32[11,1056,120]{2,1,0:T(8,128)S(1)}, f32[12,44,240]{2,1,0:T(8,128)S(1)}, f32[12,960]{1,0:T(8,128)S(1)}) custom-call(f32[11,12,1056]{2,1,0:T(8,128)} %occ.1, f32[11,1056,120]{2,1,0:T(8,128)} %bitcast.5, f32[12,960]{1,0:T(8,128)} %sing.1), custom_call_target="tpu_custom_call" | custom-call | tf_op jit(solution)/shard_map/dress/pallas_call | solution.py:371
  55.9 2.6 %copy.9 = f32[11,120,1056]{1,2,0:T(8,128)} copy(f32[11,120,1056]{1,2,0:T(8,128)S(1)} %bitcast.3) | data formatting | bytes 11151360
  58.5 0.8 %copy.10 = f32[44,12,240]{2,0,1:T(8,128)} copy(f32[44,12,240]{2,0,1:T(8,128)S(1)} %bitcast.4) | data formatting | bytes 1013760
  59.3 0.6 %copy.11 = f32[12,960]{1,0:T(8,128)} copy(f32[12,960]{1,0:T(8,128)S(1)} %get-tuple-element.14) | data formatting | bytes 92160

commit v4 on v3

--- a/solution.py
+++ b/solution.py
@@ -9,8 +9,8 @@
 F32, BF16 = jnp.float32, jnp.bfloat16
 LANES = 128
 CORES = 2
-SKEW = 2
-AHEAD = 4
+SKEW = 1
+AHEAD = 5
 
 
 def split(x):
@@ -43,7 +43,7 @@
     def kernel(occ, vir, sing, out_vir, out_ov, out_fock,
                gath, amps, tails, vloc, oloc, sloc, xbuf, drows, tmat, tright, sleft, lwts,
                ovsend, ovrecv, ovout, fbuf, fout,
-               s_right, s_left, s_part, r_sem, ov_s, ov_r, f_s, f_r, in_sem, v_in, v_out, o_out):
+               s_right, s_left, s_part, r_sem, a_s, a_r, ov_s, ov_r, f_s, f_r, in_sem, v_in, v_out, o_out):
         v = lax.axis_index("vec")
         o = lax.axis_index("orb")
         z = o // CORES
@@ -65,10 +65,6 @@
         def vout(q):
             return pltpu.make_async_copy(vloc.at[q], out_vir.at[q], v_out.at[q])
 
-        @pl.loop(0, Q)
-        def _(q):
-            vin(q).start()
-
         bar = pltpu.get_barrier_semaphore()
 
         @pl.when(has_r)
@@ -85,8 +81,12 @@
 
         c_occ.wait()
         c_sing.wait()
-        for j in range(NJ):
-            amps[o, j] = sloc[j * GR:(j + 1) * GR, :]
+        for w in range(W):
+            @pl.when(v == w)
+            def _():
+                cols = sloc[:, w * PIECE:(w + 1) * PIECE]
+                for j in range(NJ):
+                    amps[w, o, j] = cols[j * GR:(j + 1) * GR]
         for q in range(Q):
             for j in range(NJ):
                 gath[o, q * NJ + j] = oloc[q, j * GR:(j + 1) * GR, 0:MAIN]
@@ -111,7 +111,7 @@
 
         def piece(d, u):
             if isinstance(u, str):
-                return {"a": amps, "t": tails}[u].at[d], {"a": Q, "t": Q + 1}[u]
+                return (amps.at[v, d], Q) if u == "a" else (tails.at[d], Q + 1)
             return gath.at[d, pl.ds(u * NJ, NJ)], u
 
         def remote(d, u, sems, target):
@@ -177,6 +177,10 @@
 
         for u in units[:AHEAD]:
             send_own(u)
+
+        @pl.loop(0, Q)
+        def _(q):
+            vin(q).start()
 
         for q in range(Q):
             for r in range(R):
@@ -190,13 +194,31 @@
                 if 0 <= n < UNITS:
                     relay(h, units[n])
         from_partner("a")
+
+        def a_copy(h):
+            w = lax.rem(v + h, W)
+            return pltpu.make_async_remote_copy(
+                src_ref=amps.at[v], dst_ref=amps.at[v], send_sem=a_s.at[h],
+                recv_sem=a_r.at[h], device_id=(w, o), device_id_type=MESH)
+
+        def a_came(h):
+            w = lax.rem(v - h + W, W)
+            return pltpu.make_async_remote_copy(
+                src_ref=amps.at[w], dst_ref=amps.at[w], send_sem=a_s.at[h],
+                recv_sem=a_r.at[h], device_id=(w, o), device_id_type=MESH)
+
+        for h in range(1, W):
+            a_copy(h).start()
         from_partner("t")
 
         xbuf[...] = jnp.zeros_like(xbuf)
+        for h in range(1, W):
+            a_came(h).wait_recv()
         for d in range(D):
             for j in range(NJ):
                 at = d * R + j * GR
-                xbuf[at:at + GR, 0:A] = amps[d, j]
+                for w in range(W):
+                    xbuf[at:at + GR, w * PIECE:(w + 1) * PIECE] = amps[w, d, j]
         amp = xbuf[0:OCC, 0:A]
         tmat[...] = jnp.zeros_like(tmat)
         shifted = jnp.concatenate([jnp.zeros((OCC, OCC), F32), amp], axis=1)
@@ -320,6 +342,7 @@
         for h in range(1, W):
             ov_copy(h).wait_send()
             f_copy(h).wait_send()
+            a_copy(h).wait_send()
         c_ov.wait()
         c_f.wait()
 
@@ -336,7 +359,7 @@
         out_specs=(any_spec,) * 3,
         scratch_shapes=[
             V((D, GRAN, GR, MAIN), F32),
-            V((D, NJ, GR, A), F32),
+            V((W, D, NJ, GR, PIECE), F32),
             V((D, GROUPS * NJ + 1, GR, LANES), F32),
             V((Q, N, RV), F32),
             V((Q, R, N), F32),
@@ -353,7 +376,7 @@
             V((W, NJ, GR, A), F32),
             V((R, A), F32),
             DMA((D, UNITS)), DMA((D, UNITS)), DMA((D, UNITS)), DMA((D, UNITS)),
-            DMA((W,)), DMA((W,)), DMA((W,)), DMA((W,)),
+            DMA((W,)), DMA((W,)), DMA((W,)), DMA((W,)), DMA((W,)), DMA((W,)),
             DMA((2,)), DMA((Q,)), DMA((Q,)), DMA((2,)),
         ],
         compiler_params=pltpu.CompilerParams(
@@ -361,6 +384,27 @@
     )
 
 
+def write_out(*refs):
+    n = (len(refs) - 1) // 2
+    copies = [pltpu.make_async_copy(refs[i], refs[n + i], refs[-1].at[i]) for i in range(n)]
+    for c in copies:
+        c.start()
+    for c in copies:
+        c.wait()
+
+
+def store(arrays):
+    return pl.pallas_call(
+        write_out,
+        name="store",
+        out_shape=tuple(jax.ShapeDtypeStruct(a.shape, a.dtype) for a in arrays),
+        in_specs=[pl.BlockSpec(memory_space=pl.ANY)] * len(arrays),
+        out_specs=(pl.BlockSpec(memory_space=pltpu.HBM),) * len(arrays),
+        scratch_shapes=[pltpu.SemaphoreType.DMA((len(arrays),))],
+        compiler_params=pltpu.CompilerParams(vmem_limit_bytes=2**20),
+    )(*arrays)
+
+
 def solution(mesh):
     W, D = mesh.shape["vec"], mesh.shape["orb"]
 
@@ -368,7 +412,7 @@
         Q, R, N = chol_occ.shape
         call = make_kernel(W, D, Q, R, chol_vir.shape[1], N, singles.shape[1])
         args = (chol_occ, jnp.swapaxes(chol_vir, 1, 2), singles)
-        vir, ov, fock = call(*(pltpu.with_memory_space_constraint(a, pltpu.HBM) for a in args))
+        vir, ov, fock = store(call(*(pltpu.with_memory_space_constraint(a, pltpu.HBM) for a in args)))
         return jnp.swapaxes(vir, 1, 2), jnp.swapaxes(ov, 0, 1), fock
 
     return jax.shard_map(

time: 60.1 us -> 60.3 us (level)
  the two profiles are of different devices: /device:TPU:0 before, /device:TPU:5 now
where the time goes in v4:
time: 60.3 us; the launch traced here: 60.1 us
  Pallas kernels  59.5 us (99%)
  between operations  0.64 us (1%)
    pallas_call x1, Pallas kernels, shards(): call(*(pltpu.with_memory_space_constraint(a, pltpu.HBM) for a in args))  56.7 us
    pallas_call x1, Pallas kernels, store(): pl.pallas_call(write_out, name='store', out_shape=tuple((jax.ShapeDtypeSt...  2.8 us

profile of v4, /device:TPU:5, one launch (start us, length us, event | category | flops | bytes accessed | tf_op | source)
XLA Modules:
  0.0 60.1 jit_solution(12797882855119316358)
XLA Ops:
  0.6 56.7 %dress.1 = (f32[11,1056,120]{2,1,0:T(8,128)S(1)}, f32[12,44,240]{2,1,0:T(8,128)S(1)}, f32[12,960]{1,0:T(8,128)S(1)}) custom-call(f32[11,12,1056]{2,1,0:T(8,128)} %occ.1, f32[11,1056,120]{2,1,0:T(8,128)} %bitcast.3, f32[12,960]{1,0:T(8,128)} %sing.1), custom_call_target="tpu_custom_call" | custom-call | tf_op jit(solution)/shard_map/dress/pallas_call | solution.py:415
  57.3 2.8 %store.1 = (f32[11,1056,120]{2,1,0:T(8,128)}, f32[12,44,240]{2,1,0:T(8,128)}, f32[12,960]{1,0:T(8,128)}) custom-call(f32[11,1056,120]{2,1,0:T(8,128)S(1)} %get-tuple-element.9.refs_0_, f32[12,44,240]{2,1,0:T(8,128)S(1)} %get-tuple-element.10.refs_1_, f32[12,960]{1,0:T(8,128)S(1)} %get-tuple-element.11.refs_2_), custom_call_target="tpu_custom_call" | custom-call | tf_op jit(solution)/shard_map/store/pallas_call | solution.py:397

commit v5 on v3

--- a/solution.py
+++ b/solution.py
@@ -9,7 +9,7 @@
 F32, BF16 = jnp.float32, jnp.bfloat16
 LANES = 128
 CORES = 2
-SKEW = 2
+SKEW = 1
 AHEAD = 4
 
 
@@ -64,10 +64,6 @@
 
         def vout(q):
             return pltpu.make_async_copy(vloc.at[q], out_vir.at[q], v_out.at[q])
-
-        @pl.loop(0, Q)
-        def _(q):
-            vin(q).start()
 
         bar = pltpu.get_barrier_semaphore()
 
@@ -177,6 +173,10 @@
 
         for u in units[:AHEAD]:
             send_own(u)
+
+        @pl.loop(0, Q)
+        def _(q):
+            vin(q).start()
 
         for q in range(Q):
             for r in range(R):
@@ -361,6 +361,27 @@
     )
 
 
+def write_out(*refs):
+    n = (len(refs) - 1) // 2
+    copies = [pltpu.make_async_copy(refs[i], refs[n + i], refs[-1].at[i]) for i in range(n)]
+    for c in copies:
+        c.start()
+    for c in copies:
+        c.wait()
+
+
+def store(arrays):
+    return pl.pallas_call(
+        write_out,
+        name="store",
+        out_shape=tuple(jax.ShapeDtypeStruct(a.shape, a.dtype) for a in arrays),
+        in_specs=[pl.BlockSpec(memory_space=pl.ANY)] * len(arrays),
+        out_specs=(pl.BlockSpec(memory_space=pltpu.HBM),) * len(arrays),
+        scratch_shapes=[pltpu.SemaphoreType.DMA((len(arrays),))],
+        compiler_params=pltpu.CompilerParams(vmem_limit_bytes=2**20),
+    )(*arrays)
+
+
 def solution(mesh):
     W, D = mesh.shape["vec"], mesh.shape["orb"]
 
@@ -368,7 +389,7 @@
         Q, R, N = chol_occ.shape
         call = make_kernel(W, D, Q, R, chol_vir.shape[1], N, singles.shape[1])
         args = (chol_occ, jnp.swapaxes(chol_vir, 1, 2), singles)
-        vir, ov, fock = call(*(pltpu.with_memory_space_constraint(a, pltpu.HBM) for a in args))
+        vir, ov, fock = store(call(*(pltpu.with_memory_space_constraint(a, pltpu.HBM) for a in args)))
         return jnp.swapaxes(vir, 1, 2), jnp.swapaxes(ov, 0, 1), fock
 
     return jax.shard_map(

time: 60.1 us -> 57.7 us (0.960)
  local copies, waits for them, and re-layouts: 4.04 us -> 0 us
  Pallas kernels: 55.3 us -> 56.9 us
    unnamed x3 -> x0, local copies, waits for them, and re-layouts: 4.04 us -> none
    pallas_call x0 -> x1, Pallas kernels: none -> 2.8 us  [store(): pl.pallas_call(write_out, name='store', out_shape=tuple((jax.ShapeDtypeSt...]
    pallas_call x1, Pallas kernels: 55.3 us -> 54.1 us  [shards(): call(*(pltpu.with_memory_space_constraint(a, pltpu.HBM) for a in args))]
where the time goes in v5:
time: 57.7 us; the launch traced here: 57.5 us
  Pallas kernels  56.9 us (99%)
  between operations  0.64 us (1%)
    pallas_call x1, Pallas kernels, shards(): call(*(pltpu.with_memory_space_constraint(a, pltpu.HBM) for a in args))  54.1 us
    pallas_call x1, Pallas kernels, store(): pl.pallas_call(write_out, name='store', out_shape=tuple((jax.ShapeDtypeSt...  2.8 us

profile of v5, /device:TPU:0, one launch (start us, length us, event | category | flops | bytes accessed | tf_op | source)
XLA Modules:
  0.0 57.5 jit_solution(17905803165476238225)
XLA Ops:
  0.6 54.1 %dress.1 = (f32[11,1056,120]{2,1,0:T(8,128)S(1)}, f32[12,44,240]{2,1,0:T(8,128)S(1)}, f32[12,960]{1,0:T(8,128)S(1)}) custom-call(f32[11,12,1056]{2,1,0:T(8,128)} %occ.1, f32[11,1056,120]{2,1,0:T(8,128)} %bitcast.3, f32[12,960]{1,0:T(8,128)} %sing.1), custom_call_target="tpu_custom_call" | custom-call | tf_op jit(solution)/shard_map/dress/pallas_call | solution.py:392
  54.7 2.8 %store.1 = (f32[11,1056,120]{2,1,0:T(8,128)}, f32[12,44,240]{2,1,0:T(8,128)}, f32[12,960]{1,0:T(8,128)}) custom-call(f32[11,1056,120]{2,1,0:T(8,128)S(1)} %get-tuple-element.9.refs_0_, f32[12,44,240]{2,1,0:T(8,128)S(1)} %get-tuple-element.10.refs_1_, f32[12,960]{1,0:T(8,128)S(1)} %get-tuple-element.11.refs_2_), custom_call_target="tpu_custom_call" | custom-call | tf_op jit(solution)/shard_map/store/pallas_call | solution.py:374
